TPU v7x, 32 devices: a whole 2x2x4 slice. The times are simulated.
32 devices in a mesh: ctx: 16 (over z, x, core), head: 2 (over y).
Axes of the slice: x: 2, y: 2, z: 4, core: 2. Of those that a mesh axis runs over, the one named last changes fastest.
Arguments:
- q_latent: bfloat16 [2048, 1536], P(('ctx', 'head')), may hold values from -320 to 320
- q_gain: float32 [1536], replicated, may hold values from 0.5 to 8
- kv_cache: bfloat16 [2048, 576], P(('ctx', 'head')), may hold values from -320 to 320
- kv_gain: float32 [512], replicated, may hold values from 0.5 to 8
- w_query: bfloat16 [1536, 12288], P(None, 'head'), may hold values from -0.15625 to 0.15625
- w_kv: bfloat16 [512, 16384], P(None, 'head'), may hold values from -0.25 to 0.25
- doc_lengths: int32 [3], replicated, may hold values from 1 to 1024, 2048 in all
Outputs:
- attn_out: bfloat16 [2048, 8192], P('ctx', 'head')
Inputs may be any that keep to these rules, and one draw needn't show every extreme that they name: `doc_lengths`: 3 documents, lengths in order summing to 2048; the longest has exactly 1024 tokens.
All inputs are finite; a program needn't handle non-finite values.
Results may differ from a plain program's by a relative error of at most 0.0075.
The roundings to bfloat16 on the way count: a program that leaves them out, or rounds other values in their place, can miss the bound.
Values may be sent and summed in bfloat16 or wider, within the bound.
A program may use at most 192 MiB of HBM per device.

v0:
```python
import functools
import math

import jax
import jax.numpy as jnp
from jax import lax
from jax.experimental import pallas as pl
from jax.experimental.pallas import tpu as pltpu
from jax.sharding import PartitionSpec as P

KL = 512
RD = 64
ND = 128
VD = 128
MESH = pl.DeviceIdType.MESH

epsilon = 1e-06


def gather_kernel(nc, nh, q_ref, kv_ref, qall_ref, win_ref, q_send, q_recv, a_send, a_recv, b_send, b_recv, c_send, c_recv):
    c = lax.axis_index("ctx")
    h = lax.axis_index("head")
    rows = kv_ref.shape[0]
    back = nc // 2
    half = back // 2
    par = lax.rem(c, 2)
    other = c + 1 - 2 * par
    head_of = [lax.rem(h + k, nh) for k in range(nh)]

    def part(slot, head):
        return win_ref.at[slot, pl.ds(pl.multiple_of(head * rows, rows), rows)]

    def qpart(head):
        return qall_ref.at[pl.ds(pl.multiple_of(head * rows, rows), rows)]

    def remote(src, dst, send, recv, ctx, head):
        return pltpu.make_async_remote_copy(
            src_ref=src, dst_ref=dst, send_sem=send, recv_sem=recv, device_id=(ctx, head), device_id_type=MESH
        )

    barrier = pltpu.get_barrier_semaphore()

    def greet(ctx, head):
        pl.semaphore_signal(barrier, inc=1, device_id=(ctx, head), device_id_type=MESH)

    for k in range(1, nh):
        greet(c, head_of[k])
    greet(other, h)
    for j in range(1, nc // 2):
        greet(lax.rem(c + 2 * j, nc), h)
    pl.semaphore_wait(barrier, nh + nc // 2 - 1)

    def q_copy(k):
        return remote(q_ref, qpart(h), q_send.at[k - 1], q_recv.at[k - 1], c, head_of[k])

    def a_copy(j):
        return remote(kv_ref, part(back - 2 * j, h), a_send.at[j - 1], a_recv.at[j - 1], c + 2 * j, h)

    def b_copy(j, k):
        src = kv_ref if j == 0 else part(back - 2 * j, h)
        return remote(src, part(back - 2 * j, h), b_send.at[j, k - 1], b_recv.at[j, k - 1], c, head_of[k])

    def c_copy(t, k, src=None):
        head = head_of[0] if k == 0 else head_of[nh - k]
        src = part(back - 2 * t - 2 * par, head) if src is None else src
        return remote(src, part(back - 2 * t - 1, head), c_send.at[t, k], c_recv.at[t, k], other, h)

    for j in range(1, half + 1):
        pl.when(c + 2 * j < nc)(lambda j=j: a_copy(j).start())
    for k in range(1, nh):
        b_copy(0, k).start()
        q_copy(k).start()

    @pl.when(par == 0)
    def _():
        c_copy(0, 0, kv_ref).start()

    win_ref[back, pl.ds(pl.multiple_of(h * rows, rows), rows)] = kv_ref[...]
    qall_ref[pl.ds(pl.multiple_of(h * rows, rows), rows)] = q_ref[...]
    for slot in range(back):
        @pl.when(c - back + slot < 0)
        def _(slot=slot):
            win_ref[slot] = jnp.zeros(win_ref.shape[1:], win_ref.dtype)

    def forward(j, k):
        if j < half:
            @pl.when(par == 0)
            def _():
                c_copy(j, k).start()
        if j > 0:
            @pl.when(par == 1)
            def _():
                c_copy(j - 1, k).start()

    for k in range(1, nh):
        b_copy(0, k).wait_recv()
        forward(0, k)
    for j in range(1, half + 1):
        @pl.when(c - 2 * j >= 0)
        def _(j=j):
            a_copy(j).wait_recv()
            for k in range(1, nh):
                b_copy(j, k).start()
            forward(j, 0)
    for j in range(1, half + 1):
        @pl.when(c - 2 * j >= 0)
        def _(j=j):
            for k in range(1, nh):
                b_copy(j, k).wait_recv()
                forward(j, k)
    for k in range(1, nh):
        q_copy(k).wait_recv()
    for t in range(half):
        @pl.when(c - 2 * t - 1 >= 0)
        def _(t=t):
            for k in range(nh):
                c_copy(t, k).wait_recv()
    for k in range(1, nh):
        q_copy(k).wait_send()
        b_copy(0, k).wait_send()
    for j in range(1, half + 1):
        pl.when(c + 2 * j < nc)(lambda j=j: a_copy(j).wait_send())

        @pl.when(c - 2 * j >= 0)
        def _(j=j):
            for k in range(1, nh):
                b_copy(j, k).wait_send()
    for t in range(half):
        @pl.when(c - 2 * t - 2 * par >= 0)
        def _(t=t):
            for k in range(nh):
                c_copy(t, k).wait_send()


def gather(q_latent, kv_cache, nc, nh):
    rows, ql = q_latent.shape
    width = kv_cache.shape[1]
    back = nc // 2
    half = back // 2
    peers = max(nh - 1, 1)
    dma = pltpu.SemaphoreType.DMA
    vmem = pl.BlockSpec(memory_space=pltpu.VMEM)
    return pl.pallas_call(
        functools.partial(gather_kernel, nc, nh),
        out_shape=(
            jax.ShapeDtypeStruct((nh * rows, ql), q_latent.dtype),
            jax.ShapeDtypeStruct((back + 1, nh * rows, width), kv_cache.dtype),
        ),
        in_specs=[vmem, vmem],
        out_specs=(vmem, vmem),
        scratch_shapes=[
            dma((peers,)), dma((peers,)), dma((half,)), dma((half,)),
            dma((half + 1, peers)), dma((half + 1, peers)), dma((half, nh)), dma((half, nh)),
        ],
        compiler_params=pltpu.CompilerParams(collective_id=0, has_side_effects=True),
        name="gather",
    )(q_latent, kv_cache)


def normed(values, gain):
    values = values.astype(jnp.float32)
    mean = jnp.mean(values * values, axis=-1, keepdims=True)
    return (values * lax.rsqrt(mean + epsilon) * gain).astype(jnp.bfloat16)


def attend_kernel(heads, first_ref, len_ref, q_ref, qg_ref, win_ref, kvg_ref, wq_ref, wkv_ref, out_ref, qn, kvn, kr, bias, cos, sin):
    tok = q_ref.shape[0]
    keys = win_ref.shape[0]
    docs = len_ref.shape[0]

    @pl.when(pl.program_id(0) == 0)
    def _():
        first = first_ref[0]
        qn[...] = normed(q_ref[...], qg_ref[...][None])
        kvn[...] = normed(win_ref[:, :KL], kvg_ref[...])
        kr[...] = win_ref[:, KL:]

        def start_of(pos):
            start = jnp.zeros_like(pos)
            end = jnp.int32(0)
            for d in range(docs):
                end = end + len_ref[d]
                start = start + jnp.where(pos >= end, len_ref[d], 0)
            return start

        qpos = first + lax.broadcasted_iota(jnp.int32, (tok, keys), 0)
        kpos = first - (keys - tok) + lax.broadcasted_iota(jnp.int32, (tok, keys), 1)
        allowed = (kpos <= qpos) & (kpos >= start_of(qpos))
        bias[...] = jnp.where(allowed, 0.0, -1e30)
        pos = first + lax.broadcasted_iota(jnp.int32, (tok, RD), 0)
        lane = lax.broadcasted_iota(jnp.int32, (tok, RD), 1)
        freq_index = jnp.where(lane < RD // 2, lane, lane - RD // 2).astype(jnp.float32)
        frequency = jnp.exp(freq_index * (-2.0 * math.log(10000.0) / RD))
        angles = (pos - start_of(pos)).astype(jnp.float32) * frequency
        cos[...] = jnp.cos(angles)
        sine = jnp.sin(angles)
        sin[...] = jnp.where(lane < RD // 2, -sine, sine)

    scale = math.log2(math.e) / math.sqrt(ND + RD)
    made = jnp.dot(qn[...], wq_ref[...], preferred_element_type=jnp.float32)

    def query_of(n):
        at = n * (ND + RD)
        turn = made[:, at + ND : at + ND + RD]
        swapped = jnp.concatenate([turn[:, RD // 2 :], turn[:, : RD // 2]], axis=1)
        turn = turn * cos[...] + swapped * sin[...]
        return jnp.concatenate([made[:, at : at + ND], turn], axis=1).astype(jnp.bfloat16)

    def expand(n):
        at = n * (ND + VD)
        return jnp.dot(
            kvn[...], wkv_ref[:, at : at + ND + VD], preferred_element_type=jnp.float32
        ).astype(jnp.bfloat16)

    def score(query, expanded):
        key = jnp.concatenate([expanded[:, :ND], kr[...]], axis=1)
        scores = lax.dot_general(query, key, (((1,), (1,)), ((), ())), preferred_element_type=jnp.float32)
        return scores + bias[...]

    expanded = [expand(n) for n in range(heads)]
    scores = [score(query_of(n), expanded[n]) for n in range(heads)]
    for n in range(heads):
        top = jnp.max(scores[n], axis=1, keepdims=True)
        weights = jnp.exp2((scores[n] - top) * scale)
        total = jnp.sum(weights, axis=1, keepdims=True)
        mixed = jnp.dot(weights.astype(jnp.bfloat16), expanded[n][:, ND:], preferred_element_type=jnp.float32)
        out_ref[:, n * VD : (n + 1) * VD] = (mixed / total).astype(jnp.bfloat16)


def attend(first, doc_lengths, q_rows, q_gain, window, kv_gain, w_query, w_kv, heads):
    tok, ql = q_rows.shape
    keys, width = window.shape
    all_heads = w_query.shape[1] // (ND + RD)
    whole = lambda shape: pl.BlockSpec(shape, lambda i, *refs: (0, 0))
    return pl.pallas_call(
        functools.partial(attend_kernel, heads),
        out_shape=jax.ShapeDtypeStruct((tok, all_heads * VD), jnp.bfloat16),
        grid_spec=pltpu.PrefetchScalarGridSpec(
            num_scalar_prefetch=2,
            grid=(all_heads // heads,),
            in_specs=[
                whole((tok, ql)),
                pl.BlockSpec((ql,), lambda i, *refs: (0,)),
                whole((keys, width)),
                whole((1, KL)),
                pl.BlockSpec((ql, heads * (ND + RD)), lambda i, *refs: (0, i)),
                pl.BlockSpec((KL, heads * (ND + VD)), lambda i, *refs: (0, i)),
            ],
            out_specs=pl.BlockSpec((tok, heads * VD), lambda i, *refs: (0, i)),
            scratch_shapes=[
                pltpu.VMEM((tok, ql), jnp.bfloat16),
                pltpu.VMEM((keys, KL), jnp.bfloat16),
                pltpu.VMEM((keys, RD), jnp.bfloat16),
                pltpu.VMEM((tok, keys), jnp.float32),
                pltpu.VMEM((tok, RD), jnp.float32),
                pltpu.VMEM((tok, RD), jnp.float32),
            ],
        ),
        compiler_params=pltpu.CompilerParams(
            dimension_semantics=("arbitrary",), vmem_limit_bytes=60 * 2**20
        ),
        name="attend",
    )(first, doc_lengths, q_rows, q_gain, window, kv_gain, w_query, w_kv)


def solution(mesh):
    nc, nh = mesh.shape["ctx"], mesh.shape["head"]

    def body(q_latent, q_gain, kv_cache, kv_gain, w_query, w_kv, doc_lengths):
        q_rows, window = gather(q_latent, kv_cache, nc, nh)
        first = (lax.axis_index("ctx") * q_rows.shape[0]).astype(jnp.int32).reshape(1)
        window = window.reshape(-1, window.shape[-1])
        return attend(first, doc_lengths, q_rows, q_gain, window, kv_gain[None], w_query, w_kv, 4)

    placed = (
        P(("ctx", "head"), None),
        P(),
        P(("ctx", "head"), None),
        P(),
        P(None, "head"),
        P(None, "head"),
        P(),
    )
    return jax.shard_map(body, mesh=mesh, in_specs=placed, out_specs=P("ctx", "head"), check_vma=False)
```

profile of v0, /device:TPU:25, one launch (start us, length us, event | category | flops | bytes accessed | tf_op | source)
XLA Modules:
  0.0 50.7 jit_solution(5478840288909928719)
XLA Ops:
  0.0 21.9 %gather.1 = (bf16[128,1536]{1,0:T(8,128)(2,1)}, bf16[9,128,576]{2,1,0:T(8,128)(2,1)}) custom-call(bf16[64,1536]{1,0:T(8,128)(2,1)} %q_ref.1, bf16[64,576]{1,0:T(8,128)(2,1)} %kv_ref.1), custom_call_target="tpu_custom_call" | custom-call | tf_op jit(solution)/shard_map/gather/pallas_call | solution.py:143
  21.9 28.8 %attend.1 = bf16[128,4096]{1,0:T(8,128)(2,1)} custom-call(s32[1]{0:T(128)} %bitcast.first_ref, s32[3]{0:T(128)} %len_ref.1, bf16[128,1536]{1,0:T(8,128)(2,1)} %get-tuple-element.7.q_ref, f32[1536]{0:T(1024)} %qg_ref.1, bf16[1152,576]{1,0:T(8,128)(2,1)} %bitcast.3, f32[1,512]{1,0:T(1,128)} %bitcast.4, bf16[1536,6144]{1,0:T(8,128)(2,1)} %wq_ref.1, ...), custom_call_target="tpu_custom_call" | custom-call | tf_op jit(solution)/shard_map/attend/pallas_call | solution.py:235
where the time goes:
time: 50.8 us; the launch traced here: 50.7 us
  Pallas kernels  50.7 us (100%)
    pallas_call x1, Pallas kernels, attend(): pl.pallas_call(functools.partial(attend_kernel, heads), out_shape=jax.Sha...  28.8 us
    pallas_call x1, Pallas kernels, gather(): pl.pallas_call(functools.partial(gather_kernel, nc, nh), out_shape=(jax.S...  21.9 us

commit v1 on v0

v1 whole, which is shorter than its diff:
```python
import functools
import math

import jax
import jax.numpy as jnp
from jax import lax
from jax.experimental import pallas as pl
from jax.experimental.pallas import tpu as pltpu
from jax.sharding import PartitionSpec as P

KL = 512
RD = 64
ND = 128
VD = 128
LANES = 128
MESH = pl.DeviceIdType.MESH

epsilon = 1e-06


def normed(values, gain):
    values = values.astype(jnp.float32)
    mean = jnp.mean(values * values, axis=-1, keepdims=True)
    return (values * lax.rsqrt(mean + epsilon) * gain).astype(jnp.bfloat16)


def attend_kernel(
    nc, nh, step, len_ref, q_ref, qg_ref, kv_ref, kvg_ref, wq_hbm, wkv_hbm, out_ref,
    wq, wkv, q_own, kv_own, q_all, win, wk_t, kv_t, kr_even, kr_odd, query, key_t, value,
    bias, cos, sin, score_a, score_b, top_a, top_b,
    wq_sem, wkv_sem, q_send, q_recv, recv, y_send, z_send, x_send, c_send,
):
    c = lax.axis_index("ctx")
    h = lax.axis_index("head")
    rows, ql = q_ref.shape
    tok = rows * nh
    back = nc // 2
    keys = (back + 1) * tok
    heads = wkv.shape[1] // (ND + VD)
    docs = len_ref.shape[0]
    par = lax.rem(c, 2)
    col = lax.rem(lax.div(c, 2), 2)
    core = c + 1 - 2 * par
    side = c + 2 - 4 * col

    def wkv_copy():
        return pltpu.make_async_copy(wkv_hbm, wkv, wkv_sem)

    q_wide = step * (ND + RD)

    def wq_copy(i):
        at = pl.ds(i * q_wide, q_wide)
        return pltpu.make_async_copy(wq_hbm.at[:, at], wq.at[:, at], wq_sem.at[i])

    wkv_copy().start()
    for i in range(heads // step):
        wq_copy(i).start()

    barrier = pltpu.get_barrier_semaphore()

    def greet(ctx, head):
        pl.semaphore_signal(barrier, inc=1, device_id=(ctx, head), device_id_type=MESH)

    for k in range(1, nh):
        greet(c, lax.rem(h + k, nh))
    greet(core, h)
    greet(side, h)
    pl.when(c + 4 < nc)(lambda: greet(c + 4, h))
    pl.when(c >= 4)(lambda: greet(c - 4, h))

    kv_own[:, :KL] = normed(kv_ref[:, :KL], kvg_ref[...])
    kv_own[:, KL:] = kv_ref[:, KL:]
    q_own[...] = normed(q_ref[...], qg_ref[...])

    pl.semaphore_wait(barrier, nh + 1 + (c + 4 < nc).astype(jnp.int32) + (c >= 4).astype(jnp.int32))

    def part_rows(k):
        return pl.ds(pl.multiple_of(lax.rem(h - k + nh, nh) * rows, rows), rows)

    def part(d, k):
        return win.at[d, part_rows(k)]

    def remote(src, dst, send, got, ctx, head):
        return pltpu.make_async_remote_copy(
            src_ref=src, dst_ref=dst, send_sem=send, recv_sem=got, device_id=(ctx, head), device_id_type=MESH
        )

    def source(d, k):
        return kv_own if d == 0 and k == 0 else part(d, k)

    def y_copy(k):
        return remote(kv_own, part(0, 0), y_send.at[k], recv.at[0, k], c, lax.rem(h + k, nh))

    def q_copy(k):
        return remote(q_own, q_all.at[part_rows(0)], q_send.at[k], q_recv.at[k], c, lax.rem(h + k, nh))

    def z_copy(d, k):
        return remote(source(d, k), part(d + 4, k), z_send.at[d // 4, k], recv.at[d + 4, k], c + 4, h)

    def x_copy(d, to, k):
        return remote(source(d, k), part(to, k), x_send.at[d // 4, k], recv.at[to, k], side, h)

    def c_copy(d, to, k):
        return remote(source(d, k), part(to, k), c_send.at[d // 2, k], recv.at[to, k], core, h)

    def onward(d, k, act):
        here = c >= d
        if d % 4 == 0:
            if d + 4 <= back:
                pl.when(here & (c + 4 < nc))(lambda: act(z_copy(d, k)))
            if d + 2 <= back:
                pl.when(here & (col == 0))(lambda: act(x_copy(d, d + 2, k)))
            if d >= 2:
                pl.when(here & (col == 1))(lambda: act(x_copy(d, d - 2, k)))
        if d % 2 == 0:
            if d + 1 <= back:
                pl.when(here & (par == 0))(lambda: act(c_copy(d, d + 1, k)))
            if d >= 1:
                pl.when(here & (par == 1))(lambda: act(c_copy(d, d - 1, k)))

    def take(d, k):
        if d == 0:
            y_copy(k).wait_recv()
        else:
            pl.when(c >= d)(lambda: remote(part(d, k), part(d, k), recv.at[d, k], recv.at[d, k], c, h).wait_recv())
        onward(d, k, lambda copy: copy.start())

    for k in range(1, nh):
        y_copy(k).start()
    onward(0, 0, lambda copy: copy.start())
    for k in range(1, nh):
        q_copy(k).start()

    win[0, part_rows(0)] = kv_own[...]
    q_all[part_rows(0)] = q_own[...]
    for d in range(1, back + 1):
        @pl.when(c < d)
        def _(d=d):
            win[d] = jnp.zeros(win.shape[1:], win.dtype)

    first = c * tok

    def start_of(pos):
        start = jnp.zeros_like(pos)
        end = jnp.int32(0)
        for d in range(docs):
            end = end + len_ref[d]
            start = start + jnp.where(pos >= end, len_ref[d], 0)
        return start

    qpos = first + lax.broadcasted_iota(jnp.int32, (tok, tok), 0)
    kcol = first + lax.broadcasted_iota(jnp.int32, (tok, tok), 1)
    start = start_of(qpos)
    for d in range(back + 1):
        kpos = kcol - d * tok
        bias[:, d * tok : (d + 1) * tok] = jnp.where((kpos <= qpos) & (kpos >= start), 0.0, -1e30)
    pos = first + lax.broadcasted_iota(jnp.int32, (tok, LANES), 0)
    lane = lax.broadcasted_iota(jnp.int32, (tok, LANES), 1)
    turn_at = lax.rem(lane, RD)
    lower = turn_at < RD // 2
    freq_index = jnp.where(lower, turn_at, turn_at - RD // 2).astype(jnp.float32)
    frequency = jnp.exp(freq_index * (-2.0 * math.log(10000.0) / RD))
    angles = (pos - start_of(pos)).astype(jnp.float32) * frequency
    cos[...] = jnp.cos(angles)
    sine = jnp.sin(angles)
    sin[...] = jnp.where(lower, -sine, sine)

    wkv_copy().wait()

    def turn_weights(i, carry):
        for odd in range(2):
            n = 2 * i + odd
            at = pl.multiple_of(n * (ND + VD), ND + VD)
            flipped = wkv[:, pl.ds(at, ND)].T
            if odd:
                flipped = jnp.concatenate([flipped[ND // 2 :], flipped[: ND // 2]], axis=0)
            wk_t[pl.ds(pl.multiple_of(n * ND, ND), ND)] = flipped
        return carry

    lax.fori_loop(0, heads // 2, turn_weights, 0)

    def expand(slots):
        wide = len(slots) * tok
        for at, d in enumerate(slots):
            kv_t[:, at * tok : (at + 1) * tok] = win[d, :, :KL].T
            rope = win[d, :, KL:]
            blank = jnp.zeros((tok, LANES - RD), rope.dtype)
            kr_even[:, d * tok : (d + 1) * tok] = jnp.concatenate([rope, blank], axis=1).T
            kr_odd[:, d * tok : (d + 1) * tok] = jnp.concatenate([blank, rope], axis=1).T
        latent = win[slots[0], :, :KL]
        if len(slots) > 1:
            latent = jnp.concatenate([win[d, :, :KL] for d in slots], axis=0)

        def some(i, carry):
            rows_at = pl.ds(pl.multiple_of(i * step * ND, step * ND), step * ND)
            made = jnp.dot(wk_t[rows_at], kv_t[:, :wide], preferred_element_type=jnp.float32).astype(jnp.bfloat16)
            for at, d in enumerate(slots):
                key_t[rows_at, d * tok : (d + 1) * tok] = made[:, at * tok : (at + 1) * tok]
            for n in range(0, step, 2):
                at = pl.multiple_of((i * step + n) * (ND + VD), 2 * (ND + VD))
                pair = jnp.concatenate(
                    [wkv[:, pl.ds(at + ND, VD)], wkv[:, pl.ds(at + 2 * ND + VD, VD)]], axis=1
                )
                made = jnp.dot(latent, pair, preferred_element_type=jnp.float32).astype(jnp.bfloat16)
                to = pl.ds(pl.multiple_of((i * step + n) * VD, 2 * VD), 2 * VD)
                for s, d in enumerate(slots):
                    value[d * tok : (d + 1) * tok, to] = made[s * tok : (s + 1) * tok]
            return carry

        lax.fori_loop(0, heads // step, some, 0)

    def project():
        def some(i, carry):
            pltpu.make_async_copy(
                wq_hbm.at[:, pl.ds(0, q_wide)], wq.at[:, pl.ds(0, q_wide)], wq_sem.at[i]
            ).wait()
            at = pl.multiple_of(i * q_wide, q_wide)
            for n in range(0, step, 2):
                off = n * (ND + RD)
                made = jnp.dot(
                    q_all[...], wq[:, pl.ds(at + off, 2 * (ND + RD))], preferred_element_type=jnp.float32
                )
                one, two, three = (made[:, j * LANES : (j + 1) * LANES] for j in range(3))
                low = lane < LANES // 2
                rope = jnp.where(low, two, three)
                other = jnp.where(lower, pltpu.roll(rope, LANES - RD // 2, 1), pltpu.roll(rope, RD // 2, 1))
                rope = rope * cos[...] + other * sin[...]
                both = jnp.concatenate([one, jnp.where(low, three, two), rope], axis=1)
                query[:, pl.ds(at + off, 2 * (ND + RD))] = both.astype(jnp.bfloat16)
            return carry

        lax.fori_loop(0, heads // step, some, 0)

    order = [0] + [d for d in range(4, back + 1, 4)] + [d for d in range(2, back + 1, 4)] + [d for d in range(1, back + 1, 2)]
    for k in range(1, nh):
        take(0, k)
    for d in range(4, back + 1, 4):
        for k in range(nh):
            take(d, k)
        if d == 4:
            expand([0, 4])
    for d in range(2, back + 1, 4):
        for k in range(nh):
            take(d, k)
    for k in range(1, nh):
        q_copy(k).wait_recv()
    project()
    for d in range(1, back + 1, 2):
        for k in range(nh):
            take(d, k)
    rest = [d for d in order if d not in (0, 4)]
    for at in range(0, len(rest), 2):
        expand(rest[at : at + 2])

    scale = math.log2(math.e) / math.sqrt(ND + RD)

    def score(m, odd, to, top):
        base = pl.multiple_of(m * 2 * (ND + RD), 2 * (ND + RD))
        left = jnp.concatenate(
            [query[:, pl.ds(base + odd * ND, ND)], query[:, pl.ds(base + 2 * ND, 2 * RD)]], axis=1
        )
        turned = kr_odd if odd else kr_even
        right = jnp.concatenate([key_t[pl.ds(pl.multiple_of((2 * m + odd) * ND, ND), ND)], turned[...]], axis=0)
        made = jnp.dot(left, right, preferred_element_type=jnp.float32) + bias[...]
        to[...] = made
        top[...] = jnp.max(made, axis=1, keepdims=True)

    def mix(n, made, top):
        weights = jnp.exp2((made[...] - top[...]) * scale)
        total = jnp.sum(weights, axis=1, keepdims=True)
        at = pl.ds(pl.multiple_of(n * VD, VD), VD)
        mixed = jnp.dot(weights.astype(jnp.bfloat16), value[:, at], preferred_element_type=jnp.float32)
        out_ref[:, at] = (mixed / total).astype(jnp.bfloat16)

    score(0, 0, score_a, top_a)

    def pair(m, carry):
        score(m, 1, score_b, top_b)
        mix(2 * m, score_a, top_a)
        score(jnp.minimum(m + 1, heads // 2 - 1), 0, score_a, top_a)
        mix(2 * m + 1, score_b, top_b)
        return carry

    lax.fori_loop(0, heads // 2, pair, 0)

    for k in range(1, nh):
        y_copy(k).wait_send()
        q_copy(k).wait_send()
    for d in range(0, back + 1, 2):
        for k in range(nh):
            onward(d, k, lambda copy: copy.wait_send())


def attend(doc_lengths, q_latent, q_gain, kv_cache, kv_gain, w_query, w_kv, nc, nh):
    rows, ql = q_latent.shape
    width = kv_cache.shape[1]
    tok = rows * nh
    back = nc // 2
    keys = (back + 1) * tok
    heads = w_kv.shape[1] // (ND + VD)
    step = min(8, heads)
    bf16, f32 = jnp.bfloat16, jnp.float32
    dma = pltpu.SemaphoreType.DMA
    vmem = pl.BlockSpec(memory_space=pltpu.VMEM)
    hbm = pl.BlockSpec(memory_space=pl.ANY)
    smem = pl.BlockSpec(memory_space=pltpu.SMEM)
    return pl.pallas_call(
        functools.partial(attend_kernel, nc, nh, step),
        out_shape=jax.ShapeDtypeStruct((tok, heads * VD), bf16),
        in_specs=[smem, vmem, vmem, vmem, vmem, hbm, hbm],
        out_specs=vmem,
        scratch_shapes=[
            pltpu.VMEM(w_query.shape, bf16),
            pltpu.VMEM(w_kv.shape, bf16),
            pltpu.VMEM((rows, ql), bf16),
            pltpu.VMEM((rows, width), bf16),
            pltpu.VMEM((tok, ql), bf16),
            pltpu.VMEM((back + 1, tok, width), bf16),
            pltpu.VMEM((heads * ND, KL), bf16),
            pltpu.VMEM((KL, 2 * tok), bf16),
            pltpu.VMEM((LANES, keys), bf16),
            pltpu.VMEM((LANES, keys), bf16),
            pltpu.VMEM((tok, heads * (ND + RD)), bf16),
            pltpu.VMEM((heads * ND, keys), bf16),
            pltpu.VMEM((keys, heads * VD), bf16),
            pltpu.VMEM((tok, keys), f32),
            pltpu.VMEM((tok, LANES), f32),
            pltpu.VMEM((tok, LANES), f32),
            pltpu.VMEM((tok, keys), f32),
            pltpu.VMEM((tok, keys), f32),
            pltpu.VMEM((tok, 1), f32),
            pltpu.VMEM((tok, 1), f32),
            dma((heads // step,)), dma, dma((nh,)), dma((nh,)), dma((back + 1, nh)), dma((nh,)),
            dma((back // 4 + 1, nh)), dma((back // 4 + 1, nh)), dma((back // 2 + 1, nh)),
        ],
        compiler_params=pltpu.CompilerParams(
            collective_id=0, has_side_effects=True, vmem_limit_bytes=67043328
        ),
        name="attend",
    )(doc_lengths, q_latent, q_gain, kv_cache, kv_gain, w_query, w_kv)


def solution(mesh):
    nc, nh = mesh.shape["ctx"], mesh.shape["head"]

    def body(q_latent, q_gain, kv_cache, kv_gain, w_query, w_kv, doc_lengths):
        return attend(doc_lengths, q_latent, q_gain[None], kv_cache, kv_gain[None], w_query, w_kv, nc, nh)

    placed = (
        P(("ctx", "head"), None),
        P(),
        P(("ctx", "head"), None),
        P(),
        P(None, "head"),
        P(None, "head"),
        P(),
    )
    return jax.shard_map(body, mesh=mesh, in_specs=placed, out_specs=P("ctx", "head"), check_vma=False)
```

time: 50.8 us -> 56.9 us (1.12)
  the two profiles are of different devices: /device:TPU:25 before, /device:TPU:16 now
where the time goes in v1:
time: 56.9 us; the launch traced here: 56.7 us
  Pallas kernels  53.1 us (93%)
  local copies, waits for them, and re-layouts  3.58 us (6%)
    pallas_call x1, Pallas kernels, attend(): pl.pallas_call(functools.partial(attend_kernel, nc, nh, step), out_shape=...  53.1 us
    unnamed x1, local copies, waits for them, and re-layouts  2.29 us
    broadcast_in_dim x1, local copies, waits for them, and re-layouts, body(): q_gain[None]  1.29 us

profile of v1, /device:TPU:16, one launch (start us, length us, event | category | flops | bytes accessed | tf_op | source)
XLA Modules:
  0.0 56.7 jit_solution(3489674469751412269)
XLA Ops:
  0.0 1.3 %broadcast_in_dim.6.qg_ref = f32[1,1536]{1,0:T(1,128)} reshape(f32[1536]{0:T(1024)} %param.8) | data formatting | bytes 12288 | tf_op jit(solution)/shard_map/broadcast_in_dim | solution.py:347
  1.3 53.1 %attend.1 = bf16[128,4096]{1,0:T(8,128)(2,1)} custom-call(s32[3]{0:T(128)} %len_ref.1, bf16[64,1536]{1,0:T(8,128)(2,1)} %q_ref.1, f32[1,1536]{1,0:T(1,128)} %broadcast_in_dim.6.qg_ref, bf16[64,576]{1,0:T(8,128)(2,1)} %kv_ref.1, f32[1,512]{1,0:T(1,128)} %bitcast.1, bf16[1536,6144]{1,0:T(8,128)(2,1)} %wq_hbm.1, bf16[512,8192]{1,0:T(8,128)(2,1)} %wkv_hbm.1), custom_call_target="tpu_custom_call" | custom-call | tf_op jit(solution)/shard_map/attend/pallas_call | solution.py:307
  54.4 2.3 %copy.9 = bf16[128,4096]{1,0:T(8,128)(2,1)} copy(bf16[128,4096]{1,0:T(8,128)(2,1)} %attend.1) | data formatting | bytes 2097152

commit v2 on v1

v2 whole, which is shorter than its diff:
```python
import functools
import math

import jax
import jax.numpy as jnp
from jax import lax
from jax.experimental import pallas as pl
from jax.experimental.pallas import tpu as pltpu
from jax.sharding import PartitionSpec as P

KL = 512
RD = 64
ND = 128
VD = 128
LANES = 128
MESH = pl.DeviceIdType.MESH

epsilon = 1e-06


def normed(values, gain):
    values = values.astype(jnp.float32)
    mean = jnp.mean(values * values, axis=-1, keepdims=True)
    return (values * lax.rsqrt(mean + epsilon) * gain).astype(jnp.bfloat16)


def attend_kernel(
    nc, nh, step, len_ref, q_ref, qg_ref, kv_ref, kvg_ref, wq_hbm, wkv_hbm, out_ref,
    wq, wkv, q_own, kv_own, q_all, win, wk_t, kv_t, rope_t, query, key_t, value,
    bias, cos, sin, scores, tops,
    wq_sem, wkv_sem, q_send, q_recv, recv, y_send, z_send, x_send,
    key_send, key_recv, value_send, value_recv, rope_send, rope_recv,
):
    c = lax.axis_index("ctx")
    h = lax.axis_index("head")
    rows, ql = q_ref.shape
    tok = rows * nh
    back = nc // 2
    heads = wkv.shape[1] // (ND + VD)
    turns = heads // step
    docs = len_ref.shape[0]
    par = lax.rem(c, 2)
    col = lax.rem(lax.div(c, 2), 2)
    core = c + 1 - 2 * par
    side = c + 2 - 4 * col

    def wkv_copy():
        return pltpu.make_async_copy(wkv_hbm, wkv, wkv_sem)

    q_wide = step * (ND + RD)

    def wq_copy(i):
        at = pl.ds(i * q_wide, q_wide)
        return pltpu.make_async_copy(wq_hbm.at[:, at], wq.at[:, at], wq_sem.at[i])

    wkv_copy().start()

    barrier = pltpu.get_barrier_semaphore()

    def greet(ctx, head):
        pl.semaphore_signal(barrier, inc=1, device_id=(ctx, head), device_id_type=MESH)

    for k in range(1, nh):
        greet(c, lax.rem(h + k, nh))
    greet(core, h)
    greet(side, h)
    pl.when(c + 4 < nc)(lambda: greet(c + 4, h))
    pl.when(c >= 4)(lambda: greet(c - 4, h))

    kv_own[:, :KL] = normed(kv_ref[:, :KL], kvg_ref[...])
    kv_own[:, KL:] = kv_ref[:, KL:]
    q_own[...] = normed(q_ref[...], qg_ref[...])

    first = c * tok

    def start_of(pos):
        start = jnp.zeros_like(pos)
        end = jnp.int32(0)
        for d in range(docs):
            end = end + len_ref[d]
            start = start + jnp.where(pos >= end, len_ref[d], 0)
        return start

    qpos = first + lax.broadcasted_iota(jnp.int32, (tok, tok), 0)
    kcol = first + lax.broadcasted_iota(jnp.int32, (tok, tok), 1)
    start = start_of(qpos)
    for d in range(back + 1):
        kpos = kcol - d * tok
        bias[:, d * tok : (d + 1) * tok] = jnp.where((kpos <= qpos) & (kpos >= start), 0.0, -1e30)
    pos = first + lax.broadcasted_iota(jnp.int32, (tok, LANES), 0)
    lane = lax.broadcasted_iota(jnp.int32, (tok, LANES), 1)
    turn_at = lax.rem(lane, RD)
    lower = turn_at < RD // 2
    freq_index = jnp.where(lower, turn_at, turn_at - RD // 2).astype(jnp.float32)
    frequency = jnp.exp(freq_index * (-2.0 * math.log(10000.0) / RD))
    angles = (pos - start_of(pos)).astype(jnp.float32) * frequency
    cos[...] = jnp.cos(angles)
    sine = jnp.sin(angles)
    sin[...] = jnp.where(lower, -sine, sine)

    wkv_copy().wait()
    for i in range(turns):
        wq_copy(i).start()

    def turn_weights(i, carry):
        for odd in range(2):
            n = 2 * i + odd
            at = pl.multiple_of(n * (ND + VD), ND + VD)
            flipped = wkv[:, pl.ds(at, ND)].T
            if odd:
                flipped = jnp.concatenate([flipped[ND // 2 :], flipped[: ND // 2]], axis=0)
            wk_t[pl.ds(pl.multiple_of(n * ND, ND), ND)] = flipped
        return carry

    lax.fori_loop(0, heads // 4, turn_weights, 0)

    pl.semaphore_wait(barrier, nh + 1 + (c + 4 < nc).astype(jnp.int32) + (c >= 4).astype(jnp.int32))

    def part_rows(k):
        return pl.ds(pl.multiple_of(lax.rem(h - k + nh, nh) * rows, rows), rows)

    def part(d, k):
        return win.at[d // 2, part_rows(k)]

    def remote(src, dst, send, got, ctx, head):
        return pltpu.make_async_remote_copy(
            src_ref=src, dst_ref=dst, send_sem=send, recv_sem=got, device_id=(ctx, head), device_id_type=MESH
        )

    def source(d, k):
        return kv_own if d == 0 and k == 0 else part(d, k)

    def y_copy(k):
        return remote(kv_own, part(0, 0), y_send.at[k], recv.at[0, k], c, lax.rem(h + k, nh))

    def q_copy(k):
        return remote(q_own, q_all.at[part_rows(0)], q_send.at[k], q_recv.at[k], c, lax.rem(h + k, nh))

    def z_copy(d, k):
        return remote(source(d, k), part(d + 4, k), z_send.at[d // 4, k], recv.at[d // 2 + 2, k], c + 4, h)

    def x_copy(d, to, k):
        return remote(source(d, k), part(to, k), x_send.at[d // 4, k], recv.at[to // 2, k], side, h)

    def onward(d, k, act):
        here = c >= d
        if d % 4 == 0:
            if d + 4 <= back:
                pl.when(here & (c + 4 < nc))(lambda: act(z_copy(d, k)))
            if d + 2 <= back:
                pl.when(here & (col == 0))(lambda: act(x_copy(d, d + 2, k)))
            if d >= 2:
                pl.when(here & (col == 1))(lambda: act(x_copy(d, d - 2, k)))

    def take(d, k):
        if d == 0:
            y_copy(k).wait_recv()
        else:
            pl.when(c >= d)(lambda: remote(part(d, k), part(d, k), recv.at[d // 2, k], recv.at[d // 2, k], c, h).wait_recv())
        onward(d, k, lambda copy: copy.start())

    for k in range(1, nh):
        y_copy(k).start()
    onward(0, 0, lambda copy: copy.start())
    for k in range(1, nh):
        q_copy(k).start()

    win[0, part_rows(0)] = kv_own[...]
    q_all[part_rows(0)] = q_own[...]
    for d in range(2, back + 1, 2):
        @pl.when(c < d)
        def _(d=d):
            win[d // 2] = jnp.zeros(win.shape[1:], win.dtype)

    lax.fori_loop(heads // 4, heads // 2, turn_weights, 0)

    def shared(d, act):
        if d == 0:
            pl.when(par == 0)(act)
        elif d == back:
            pl.when(par == 1)(act)
        else:
            act()

    def key_rows(i):
        return pl.ds(pl.multiple_of(i * step * ND, step * ND), step * ND)

    def value_cols(i):
        return pl.ds(pl.multiple_of(i * step * VD, step * VD), step * VD)

    def copies(d, i):
        to = d + 1 - 2 * par
        at = lax.div(to, 2)
        return (
            remote(key_t.at[d, key_rows(i)], key_t.at[to, key_rows(i)], key_send.at[d // 2, i], key_recv.at[at, i], core, h),
            remote(
                value.at[d, :, value_cols(i)], value.at[to, :, value_cols(i)],
                value_send.at[d // 2, i], value_recv.at[at, i], core, h,
            ),
        )

    def rope_copy(d):
        to = d + 1 - 2 * par
        return remote(rope_t.at[d], rope_t.at[to], rope_send.at[d // 2], rope_recv.at[lax.div(to, 2)], core, h)

    def share(d, i):
        def act():
            for copy in copies(d, i):
                copy.start()

        shared(d, act)

    def expand(slots):
        wide = len(slots) * tok
        for at, d in enumerate(slots):
            kv_t[:, at * tok : (at + 1) * tok] = win[d // 2, :, :KL].T
            rope = win[d // 2, :, KL:]
            rope_t[d] = jnp.concatenate([rope, jnp.zeros((tok, LANES - RD), rope.dtype)], axis=1).T

        def some(i):
            made = jnp.dot(wk_t[key_rows(i)], kv_t[:, :wide], preferred_element_type=jnp.float32).astype(jnp.bfloat16)
            for at, d in enumerate(slots):
                key_t[d, key_rows(i)] = made[:, at * tok : (at + 1) * tok]
            latent = [win[d // 2, :, :KL] for d in slots]
            latent = jnp.concatenate(latent, axis=0) if len(slots) > 1 else latent[0]
            for n in range(0, step, 2):
                at = pl.multiple_of((i * step + n) * (ND + VD), 2 * (ND + VD))
                pair = jnp.concatenate(
                    [wkv[:, pl.ds(at + ND, VD)], wkv[:, pl.ds(at + 2 * ND + VD, VD)]], axis=1
                )
                made = jnp.dot(latent, pair, preferred_element_type=jnp.float32).astype(jnp.bfloat16)
                to = pl.ds(pl.multiple_of((i * step + n) * VD, 2 * VD), 2 * VD)
                for at, d in enumerate(slots):
                    value[d, :, to] = made[at * tok : (at + 1) * tok]

        def later(i, carry):
            some(i)
            for d in slots:
                share(d, i - 1)
            return carry

        some(0)
        for d in slots:
            shared(d, lambda d=d: rope_copy(d).start())
        lax.fori_loop(1, turns, later, 0)
        return lambda: [share(d, turns - 1) for d in slots]

    def project(begin, end):
        def some(i, carry):
            pltpu.make_async_copy(
                wq_hbm.at[:, pl.ds(0, q_wide)], wq.at[:, pl.ds(0, q_wide)], wq_sem.at[i]
            ).wait()
            at = pl.multiple_of(i * q_wide, q_wide)
            for n in range(0, step, 2):
                off = n * (ND + RD)
                made = jnp.dot(
                    q_all[...], wq[:, pl.ds(at + off, 2 * (ND + RD))], preferred_element_type=jnp.float32
                )
                one, two, three = (made[:, j * LANES : (j + 1) * LANES] for j in range(3))
                low = lane < LANES // 2
                rope = jnp.where(low, two, three)
                other = jnp.where(lower, pltpu.roll(rope, LANES - RD // 2, 1), pltpu.roll(rope, RD // 2, 1))
                rope = rope * cos[...] + other * sin[...]
                both = jnp.concatenate([one, jnp.where(low, three, two), rope], axis=1)
                query[:, pl.ds(at + off, 2 * (ND + RD))] = both.astype(jnp.bfloat16)
            return carry

        lax.fori_loop(begin, end, some, 0)

    column = list(range(0, back + 1, 4))
    beside = list(range(2, back + 1, 4))
    for k in range(1, nh):
        take(0, k)
    for k in range(nh):
        take(4, k)
    early = 8 <= back
    if early:
        take(8, 0)
    last = expand([0, 4])
    for d in column[2:]:
        for k in range(1 if early and d == 8 else 0, nh):
            take(d, k)
    for k in range(1, nh):
        q_copy(k).wait_recv()
    last()
    project(0, turns // 2)
    rest = beside[:1] + column[2:] + beside[1:]
    for at in range(0, len(rest), 2):
        slots = rest[at : at + 2]
        for d in slots:
            if d in beside:
                for k in range(nh):
                    take(d, k)
        if at:
            last()
        last = expand(slots)
    project(turns // 2, turns - 1)
    last()
    project(turns - 1, turns)

    def arrived(i):
        for d in range(0, back, 2):
            for ref, sem in ((key_t.at[d + 1, key_rows(i)], key_recv), (value.at[d + 1, :, value_cols(i)], value_recv)):
                remote(ref, ref, sem.at[d // 2, i], sem.at[d // 2, i], core, h).wait_recv()

    for d in range(0, back, 2):
        ref = rope_t.at[d + 1]
        remote(ref, ref, rope_recv.at[d // 2], rope_recv.at[d // 2], core, h).wait_recv()
    arrived(0)

    scale = math.log2(math.e) / math.sqrt(ND + RD)

    slots = range(back + 1)

    def score(m, at):
        base = pl.multiple_of(m * 2 * (ND + RD), 2 * (ND + RD))
        for odd in range(2):
            left = jnp.concatenate(
                [query[:, pl.ds(base + odd * ND, ND)], query[:, pl.ds(base + 2 * ND, 2 * RD)]], axis=1
            )
            rows_at = pl.ds(pl.multiple_of((2 * m + odd) * ND, ND), ND)
            plain = jnp.concatenate([key_t[d, rows_at] for d in slots], axis=1)
            rope = jnp.concatenate([rope_t[d] for d in slots], axis=1)
            parts = [plain, rope[RD:], rope[:RD]] if odd else [plain, rope]
            made = jnp.dot(left, jnp.concatenate(parts, axis=0), preferred_element_type=jnp.float32) + bias[...]
            scores[2 * at + odd][...] = made
            tops[2 * at + odd][...] = jnp.max(made, axis=1, keepdims=True)

    def mix(m, at):
        for odd in range(2):
            weights = jnp.exp2((scores[2 * at + odd][...] - tops[2 * at + odd][...]) * scale)
            total = jnp.sum(weights, axis=1, keepdims=True)
            cols = pl.ds(pl.multiple_of((2 * m + odd) * VD, VD), VD)
            values = jnp.concatenate([value[d, :, cols] for d in slots], axis=0)
            mixed = jnp.dot(weights.astype(jnp.bfloat16), values, preferred_element_type=jnp.float32)
            out_ref[:, cols] = (mixed / total).astype(jnp.bfloat16)

    score(0, 0)
    per = step // 4

    def four(t, carry):
        @pl.when((lax.rem(t + 1, per) == 0) & (t + 1 < heads // 4))
        def _():
            arrived(lax.div(t + 1, per))

        score(2 * t + 1, 1)
        mix(2 * t, 0)
        score(jnp.minimum(2 * t + 2, heads // 2 - 1), 0)
        mix(2 * t + 1, 1)
        return carry

    lax.fori_loop(0, heads // 4, four, 0)

    for k in range(1, nh):
        y_copy(k).wait_send()
        q_copy(k).wait_send()
    for d in range(0, back + 1, 2):
        for k in range(nh):
            onward(d, k, lambda copy: copy.wait_send())

        def sent(d=d):
            rope_copy(d).wait_send()
            for i in range(turns):
                for copy in copies(d, i):
                    copy.wait_send()

        shared(d, sent)


def attend(doc_lengths, q_latent, q_gain, kv_cache, kv_gain, w_query, w_kv, nc, nh):
    rows, ql = q_latent.shape
    width = kv_cache.shape[1]
    tok = rows * nh
    back = nc // 2
    keys = (back + 1) * tok
    heads = w_kv.shape[1] // (ND + VD)
    step = min(8, heads)
    turns = heads // step
    even = back // 2 + 1
    bf16, f32 = jnp.bfloat16, jnp.float32
    dma = pltpu.SemaphoreType.DMA
    vmem = pl.BlockSpec(memory_space=pltpu.VMEM)
    hbm = pl.BlockSpec(memory_space=pl.ANY)
    smem = pl.BlockSpec(memory_space=pltpu.SMEM)
    return pl.pallas_call(
        functools.partial(attend_kernel, nc, nh, step),
        out_shape=jax.ShapeDtypeStruct((tok, heads * VD), bf16),
        in_specs=[smem, vmem, vmem, vmem, vmem, hbm, hbm],
        out_specs=vmem,
        scratch_shapes=[
            pltpu.VMEM(w_query.shape, bf16),
            pltpu.VMEM(w_kv.shape, bf16),
            pltpu.VMEM((rows, ql), bf16),
            pltpu.VMEM((rows, width), bf16),
            pltpu.VMEM((tok, ql), bf16),
            pltpu.VMEM((even, tok, width), bf16),
            pltpu.VMEM((heads * ND, KL), bf16),
            pltpu.VMEM((KL, 2 * tok), bf16),
            pltpu.VMEM((back + 1, LANES, tok), bf16),
            pltpu.VMEM((tok, heads * (ND + RD)), bf16),
            pltpu.VMEM((back + 1, heads * ND, tok), bf16),
            pltpu.VMEM((back + 1, tok, heads * VD), bf16),
            pltpu.VMEM((tok, keys), f32),
            pltpu.VMEM((tok, LANES), f32),
            pltpu.VMEM((tok, LANES), f32),
            [pltpu.VMEM((tok, keys), f32)] * 4,
            [pltpu.VMEM((tok, 1), f32)] * 4,
            dma((turns,)), dma, dma((nh,)), dma((nh,)), dma((even, nh)), dma((nh,)), dma((even, nh)), dma((even, nh)),
            dma((even, turns)), dma((even, turns)), dma((even, turns)), dma((even, turns)), dma((even,)), dma((even,)),
        ],
        compiler_params=pltpu.CompilerParams(
            collective_id=0, has_side_effects=True, vmem_limit_bytes=67043328
        ),
        name="attend",
    )(doc_lengths, q_latent, q_gain, kv_cache, kv_gain, w_query, w_kv)


def solution(mesh):
    nc, nh = mesh.shape["ctx"], mesh.shape["head"]

    def body(q_latent, q_gain, kv_cache, kv_gain, w_query, w_kv, doc_lengths):
        return attend(doc_lengths, q_latent, q_gain[None], kv_cache, kv_gain[None], w_query, w_kv, nc, nh)

    placed = (
        P(("ctx", "head"), None),
        P(),
        P(("ctx", "head"), None),
        P(),
        P(None, "head"),
        P(None, "head"),
        P(),
    )
    return jax.shard_map(body, mesh=mesh, in_specs=placed, out_specs=P("ctx", "head"), check_vma=False)
```

time: 56.9 us -> 45.6 us (0.80)
  Pallas kernels: 53.1 us -> 41.7 us
    pallas_call x1, Pallas kernels: 53.1 us -> 41.7 us  [attend(): pl.pallas_call(functools.partial(attend_kernel, nc, nh, step), out_shape=...]
where the time goes in v2:
time: 45.6 us; the launch traced here: 45.3 us
  Pallas kernels  41.7 us (91%)
  local copies, waits for them, and re-layouts  3.58 us (8%)
    pallas_call x1, Pallas kernels, attend(): pl.pallas_call(functools.partial(attend_kernel, nc, nh, step), out_shape=...  41.7 us
    unnamed x1, local copies, waits for them, and re-layouts  2.29 us
    broadcast_in_dim x1, local copies, waits for them, and re-layouts, body(): q_gain[None]  1.29 us

profile of v2, /device:TPU:16, one launch (start us, length us, event | category | flops | bytes accessed | tf_op | source)
XLA Modules:
  0.0 45.3 jit_solution(12140972716064511148)
XLA Ops:
  0.0 1.3 %broadcast_in_dim.6.qg_ref = f32[1,1536]{1,0:T(1,128)} reshape(f32[1536]{0:T(1024)} %param.8) | data formatting | bytes 12288 | tf_op jit(solution)/shard_map/broadcast_in_dim | solution.py:422
  1.3 41.7 %attend.1 = bf16[128,4096]{1,0:T(8,128)(2,1)} custom-call(s32[3]{0:T(128)} %len_ref.1, bf16[64,1536]{1,0:T(8,128)(2,1)} %q_ref.1, f32[1,1536]{1,0:T(1,128)} %broadcast_in_dim.6.qg_ref, bf16[64,576]{1,0:T(8,128)(2,1)} %kv_ref.1, f32[1,512]{1,0:T(1,128)} %bitcast.1, bf16[1536,6144]{1,0:T(8,128)(2,1)} %wq_hbm.1, bf16[512,8192]{1,0:T(8,128)(2,1)} %wkv_hbm.1), custom_call_target="tpu_custom_call" | custom-call | tf_op jit(solution)/shard_map/attend/pallas_call | solution.py:385
  43.0 2.3 %copy.9 = bf16[128,4096]{1,0:T(8,128)(2,1)} copy(bf16[128,4096]{1,0:T(8,128)(2,1)} %attend.1) | data formatting | bytes 2097152
